TPU v7x, 32 devices: a whole 2x2x4 slice. The times are simulated.
32 devices in a mesh: seq: 2 (over y), shard: 4 (over x, core), rep: 4 (over z).
Axes of the slice: x: 2, y: 2, z: 4, core: 2. Of those that a mesh axis runs over, the one named last changes fastest.
Arguments:
- tokens: bfloat16 [16, 580, 1024], P(('shard', 'rep'), 'seq'), may hold values from -6 to 6
- lengths: int32 [16], P(('shard', 'rep')), may hold values from 435 to 580, as said below
- qkv_weight: bfloat16 [1024, 3072], P('shard'), may hold values from -0.1875 to 0.1875
- query_bias: bfloat16 [1024], P('shard'), may hold values from -3 to 3
- value_bias: bfloat16 [1024], P('shard'), may hold values from -0.29882812 to 0.29882812
- out_weight: bfloat16 [1024, 1024], P('shard'), may hold values from -2 to 2
- out_bias: bfloat16 [1024], P('shard'), may hold values from -0.59765625 to 0.59765625
- first_gain: bfloat16 [1024], P('shard'), may hold values from 0.5 to 1.5
- first_shift: bfloat16 [1024], P('shard'), may hold values from -0.29882812 to 0.29882812
- second_gain: bfloat16 [1024], P('shard'), may hold values from 0.5 to 1.5
- second_shift: bfloat16 [1024], P('shard'), may hold values from -3 to 3
- up_weight: bfloat16 [1024, 4096], P('shard'), may hold values from -0.1875 to 0.1875
- up_bias: bfloat16 [4096], P('shard'), may hold values from -3 to 3
- down_weight: bfloat16 [4096, 1024], P('shard'), may hold values from -0.09375 to 0.09375
- down_bias: bfloat16 [1024], P('shard'), may hold values from -3 to 3
- cotangent: bfloat16 [16, 580, 1024], P(('shard', 'rep'), 'seq'), may hold values from -6 to 6
Outputs:
- block_out: bfloat16 [16, 580, 1024], P(('shard', 'rep'), 'seq')
- token_grad: float32 [16, 580, 1024], P(('shard', 'rep'), 'seq')
- grad_qkv_weight: float32 [1024, 3072], P('shard')
- grad_query_bias: float32 [1024], P('shard')
- grad_value_bias: float32 [1024], P('shard')
- grad_out_weight: float32 [1024, 1024], P('shard')
- grad_out_bias: float32 [1024], P('shard')
- grad_first_gain: float32 [1024], P('shard')
- grad_first_shift: float32 [1024], P('shard')
- grad_second_gain: float32 [1024], P('shard')
- grad_second_shift: float32 [1024], P('shard')
- grad_up_weight: float32 [1024, 4096], P('shard')
- grad_up_bias: float32 [4096], P('shard')
- grad_down_weight: float32 [4096, 1024], P('shard')
- grad_down_bias: float32 [1024], P('shard')
Inputs may be any that keep to these rules, and one draw needn't show every extreme that they name: Tokens of an image at positions lengths[image] and beyond are padding. Some image has 580 valid tokens and some has 435.
All inputs are finite; a program needn't handle non-finite values.
Results may differ from a plain program's by a relative error of at most 0.012.
Values may be sent and summed in bfloat16 or wider, within the bound.
No kernel may reach another device: no remote copies, remote signals or barrier semaphores. Data moves between devices by JAX's collectives and lax.ppermute only.
A program may use at most 192 MiB of HBM per device.

v0:
```python
import jax
import jax.numpy as jnp
from jax import lax
from jax.sharding import PartitionSpec as P

H = 16
HD = 64


def layer_norm(values, gain_vec, shift_vec):
    centered = values - jnp.mean(values, -1, keepdims=True)
    variance = jnp.mean(centered * centered, -1, keepdims=True)
    return centered * lax.rsqrt(variance + 1e-06) * gain_vec + shift_vec


def gelu_exact(values):
    return jax.nn.gelu(values, approximate=False)


def attention_scores(query_heads, key_heads, visible, score_scale):
    scores = (
        jnp.einsum("iqhd,ikhd->ihqk", query_heads, key_heads, preferred_element_type=jnp.float32)
        * score_scale
    )
    return jnp.where(visible[:, None, None, :], scores, -1000000000.0)


def single_out(values):
    return values.reshape((values.shape[0], 1) + values.shape[1:])


def merge_out(values):
    return values.reshape((values.shape[0] * values.shape[1],) + values.shape[2:])


def shards(
    tokens,
    lengths,
    qkv_weight,
    query_bias,
    value_bias,
    out_weight,
    out_bias,
    first_gain,
    first_shift,
    second_gain,
    second_shift,
    up_weight,
    up_bias,
    down_weight,
    down_bias,
    cotangent,
):
    images, rows_local, model_width = tokens.shape
    full_len = rows_local * lax.axis_size("seq")
    score_scale = HD ** (-0.5)
    gathered = (
        lax.all_gather(qkv_weight, "shard", axis=0, tiled=True),
        lax.all_gather(out_weight, "shard", axis=0, tiled=True),
        lax.all_gather(up_weight, "shard", axis=0, tiled=True),
        lax.all_gather(down_weight, "shard", axis=0, tiled=True),
        lax.all_gather(query_bias, "shard", axis=0, tiled=True),
        lax.all_gather(value_bias, "shard", axis=0, tiled=True),
        lax.all_gather(out_bias, "shard", axis=0, tiled=True),
        lax.all_gather(first_gain, "shard", axis=0, tiled=True),
        lax.all_gather(first_shift, "shard", axis=0, tiled=True),
        lax.all_gather(second_gain, "shard", axis=0, tiled=True),
        lax.all_gather(second_shift, "shard", axis=0, tiled=True),
        lax.all_gather(up_bias, "shard", axis=0, tiled=True),
        lax.all_gather(down_bias, "shard", axis=0, tiled=True),
    )
    wqkv, wout, wup, wdown = (gathered[0], gathered[1], gathered[2], gathered[3])
    vec_query, vec_value, vec_out, gain_one, shift_one, gain_two, shift_two, vec_up, vec_down = [
        item.astype(jnp.float32) for item in gathered[4:]
    ]
    flat_rows = tokens.reshape(-1, model_width).astype(jnp.float32)
    normed_first, pull_first = jax.vjp(layer_norm, flat_rows, gain_one, shift_one)
    first_low = normed_first.astype(jnp.bfloat16)
    projected = jnp.dot(first_low, wqkv, preferred_element_type=jnp.float32)
    queries = (projected[:, :model_width] + vec_query).astype(jnp.bfloat16)
    keys_local = projected[:, model_width : 2 * model_width].astype(jnp.bfloat16)
    values_local = (projected[:, 2 * model_width :] + vec_value).astype(jnp.bfloat16)
    keys_all, values_all = (
        lax.all_gather(
            keys_local.reshape(images, rows_local, model_width), "seq", axis=1, tiled=True
        ),
        lax.all_gather(
            values_local.reshape(images, rows_local, model_width), "seq", axis=1, tiled=True
        ),
    )
    query_heads = single_out(queries.reshape(images, rows_local, H, HD))
    key_heads = single_out(keys_all.reshape(images, full_len, H, HD))
    value_heads = single_out(values_all.reshape(images, full_len, H, HD))
    visible = single_out(jnp.arange(full_len, dtype=jnp.int32)[None, :] < lengths[:, None])

    def attend_forward(block):
        query_blk, key_blk, value_blk, visible_blk = block
        scores = attention_scores(query_blk, key_blk, visible_blk, score_scale)
        score_top = jnp.max(scores, -1, keepdims=True)
        shifted = jnp.exp(scores - score_top)
        exp_total = jnp.sum(shifted, -1, keepdims=True)
        log_total = score_top + jnp.log(exp_total)
        weights_low = (shifted / exp_total).astype(jnp.bfloat16)
        mixed_blk = jnp.einsum(
            "ihqk,ikhd->iqhd", weights_low, value_blk, preferred_element_type=jnp.float32
        )
        return (mixed_blk.astype(jnp.bfloat16), log_total)

    mixed_out, log_totals = lax.map(attend_forward, (query_heads, key_heads, value_heads, visible))
    mixed_low = mixed_out.reshape(-1, model_width)
    middle = flat_rows + jnp.dot(mixed_low, wout, preferred_element_type=jnp.float32) + vec_out
    normed_second, pull_second = jax.vjp(layer_norm, middle, gain_two, shift_two)
    second_low = normed_second.astype(jnp.bfloat16)
    hidden = jnp.dot(second_low, wup, preferred_element_type=jnp.float32) + vec_up
    activated, pull_gelu = jax.vjp(gelu_exact, hidden)
    act_low = activated.astype(jnp.bfloat16)
    result = middle + jnp.dot(act_low, wdown, preferred_element_type=jnp.float32) + vec_down
    block_out = result.astype(jnp.bfloat16).reshape(tokens.shape)
    back_qkv, back_out, back_up, back_down = (
        lax.all_gather(qkv_weight, "shard", axis=0, tiled=True),
        lax.all_gather(out_weight, "shard", axis=0, tiled=True),
        lax.all_gather(up_weight, "shard", axis=0, tiled=True),
        lax.all_gather(down_weight, "shard", axis=0, tiled=True),
    )
    incoming = cotangent.reshape(-1, model_width)
    incoming_f = incoming.astype(jnp.float32)
    grad_down = jnp.dot(act_low.T, incoming, preferred_element_type=jnp.float32)
    grad_down_bias = jnp.sum(incoming_f, 0)
    grad_act = jnp.dot(incoming, back_down.T, preferred_element_type=jnp.float32)
    hidden_low = pull_gelu(grad_act)[0].astype(jnp.bfloat16)
    grad_up = jnp.dot(second_low.T, hidden_low, preferred_element_type=jnp.float32)
    grad_up_bias = jnp.sum(hidden_low.astype(jnp.float32), 0)
    grad_second = jnp.dot(hidden_low, back_up.T, preferred_element_type=jnp.float32)
    middle_norm, grad_gain_two, grad_shift_two = pull_second(grad_second)
    grad_middle = incoming_f + middle_norm
    branch_low = grad_middle.astype(jnp.bfloat16)
    grad_out = jnp.dot(mixed_low.T, branch_low, preferred_element_type=jnp.float32)
    grad_out_bias = jnp.sum(branch_low.astype(jnp.float32), 0)
    grad_mixed = (
        jnp.dot(branch_low, back_out.T, preferred_element_type=jnp.float32)
        .astype(jnp.bfloat16)
        .reshape(images, rows_local, H, HD)
    )

    def attend_backward(block):
        query_blk, key_blk, value_blk, visible_blk, mixed_grad_blk, log_blk = block
        scores = attention_scores(query_blk, key_blk, visible_blk, score_scale)
        weights_exact = jnp.exp(scores - log_blk)
        grad_weights = jnp.einsum(
            "iqhd,ikhd->ihqk", mixed_grad_blk, value_blk, preferred_element_type=jnp.float32
        )
        row_inner = jnp.sum(weights_exact * grad_weights, -1, keepdims=True)
        grad_scores = (weights_exact * (grad_weights - row_inner)).astype(jnp.bfloat16)
        query_grad_blk = (
            jnp.einsum("ihqk,ikhd->iqhd", grad_scores, key_blk, preferred_element_type=jnp.float32)
            * score_scale
        )
        key_blk_part = (
            jnp.einsum(
                "ihqk,iqhd->ikhd", grad_scores, query_blk, preferred_element_type=jnp.float32
            )
            * score_scale
        )
        value_blk_part = jnp.einsum(
            "ihqk,iqhd->ikhd",
            weights_exact.astype(jnp.bfloat16),
            mixed_grad_blk,
            preferred_element_type=jnp.float32,
        )
        return (query_grad_blk, key_blk_part, value_blk_part)

    grad_queries, key_part, value_part = lax.map(
        attend_backward,
        (query_heads, key_heads, value_heads, visible, single_out(grad_mixed), log_totals),
    )
    key_part = merge_out(key_part)
    value_part = merge_out(value_part)
    grad_keys, grad_values = (
        lax.psum_scatter(key_part, "seq", scatter_dimension=1, tiled=True),
        lax.psum_scatter(value_part, "seq", scatter_dimension=1, tiled=True),
    )
    query_low = grad_queries.reshape(-1, model_width).astype(jnp.bfloat16)
    value_low = grad_values.reshape(-1, model_width).astype(jnp.bfloat16)
    grad_proj = jnp.concatenate(
        [query_low, grad_keys.reshape(-1, model_width).astype(jnp.bfloat16), value_low], axis=1
    )
    grad_qkv = jnp.dot(first_low.T, grad_proj, preferred_element_type=jnp.float32)
    grad_query_bias = jnp.sum(query_low.astype(jnp.float32), 0)
    grad_value_bias = jnp.sum(value_low.astype(jnp.float32), 0)
    grad_first = jnp.dot(grad_proj, back_qkv.T, preferred_element_type=jnp.float32)
    flat_norm, grad_gain_one, grad_shift_one = pull_first(grad_first)
    token_grad = (grad_middle + flat_norm).reshape(tokens.shape)
    owned_grads = (
        lax.psum_scatter(grad_qkv, "shard", scatter_dimension=0, tiled=True),
        lax.psum_scatter(grad_query_bias, "shard", scatter_dimension=0, tiled=True),
        lax.psum_scatter(grad_value_bias, "shard", scatter_dimension=0, tiled=True),
        lax.psum_scatter(grad_out, "shard", scatter_dimension=0, tiled=True),
        lax.psum_scatter(grad_out_bias, "shard", scatter_dimension=0, tiled=True),
        lax.psum_scatter(grad_gain_one, "shard", scatter_dimension=0, tiled=True),
        lax.psum_scatter(grad_shift_one, "shard", scatter_dimension=0, tiled=True),
        lax.psum_scatter(grad_gain_two, "shard", scatter_dimension=0, tiled=True),
        lax.psum_scatter(grad_shift_two, "shard", scatter_dimension=0, tiled=True),
        lax.psum_scatter(grad_up, "shard", scatter_dimension=0, tiled=True),
        lax.psum_scatter(grad_up_bias, "shard", scatter_dimension=0, tiled=True),
        lax.psum_scatter(grad_down, "shard", scatter_dimension=0, tiled=True),
        lax.psum_scatter(grad_down_bias, "shard", scatter_dimension=0, tiled=True),
    )
    summed = lax.psum(
        (
            owned_grads[0],
            owned_grads[1],
            owned_grads[2],
            owned_grads[3],
            owned_grads[4],
            owned_grads[5],
            owned_grads[6],
            owned_grads[7],
            owned_grads[8],
            owned_grads[9],
            owned_grads[10],
            owned_grads[11],
            owned_grads[12],
        ),
        ("seq", "rep"),
    )
    return (
        block_out,
        token_grad,
        summed[0],
        summed[1],
        summed[2],
        summed[3],
        summed[4],
        summed[5],
        summed[6],
        summed[7],
        summed[8],
        summed[9],
        summed[10],
        summed[11],
        summed[12],
    )


def solution(mesh):
    return jax.shard_map(
        shards,
        mesh=mesh,
        in_specs=(
            P(("shard", "rep"), "seq", None),
            P(("shard", "rep")),
            P("shard", None),
            P("shard"),
            P("shard"),
            P("shard", None),
            P("shard"),
            P("shard"),
            P("shard"),
            P("shard"),
            P("shard"),
            P("shard", None),
            P("shard"),
            P("shard", None),
            P("shard"),
            P(("shard", "rep"), "seq", None),
        ),
        out_specs=(
            P(("shard", "rep"), "seq", None),
            P(("shard", "rep"), "seq", None),
            P("shard", None),
            P("shard"),
            P("shard"),
            P("shard", None),
            P("shard"),
            P("shard"),
            P("shard"),
            P("shard"),
            P("shard"),
            P("shard", None),
            P("shard"),
            P("shard", None),
            P("shard"),
        ),
        check_vma=False,
    )
```

profile of v0, /device:TPU:0, one launch (start us, length us, event | category | flops | bytes accessed | tf_op | source)
XLA Modules:
  0.0 1235.9 jit_solution(14504747822557526560)
XLA Ops:
  9.3 6.0 all-gather.3
  15.3 5.4 all-gather.2
  23.4 35.2 %all-gather.19.cloned.1.call-done = bf16[1024,3072]{1,0:T(8,128)(2,1)} async-done(((bf16[256,3072]{1,0:T(8,128)(2,1)}), bf16[1024,3072]{1,0:T(8,128)(2,1)}) %all-gather.19.cloned.1.call-update) | async-done | bytes 6291472 | tf_op jit(solution)/shard_map/all_gather | solution.py:58
  97.5 5.7 all_gather.61
  142.1 56.9 %all-gather.23.cloned.1.call-done = bf16[1024,4096]{1,0:T(8,128)(2,1)} async-done(((bf16[256,4096]{1,0:T(8,128)(2,1)}), bf16[1024,4096]{1,0:T(8,128)(2,1)}) %all-gather.23.cloned.1.call-update) | async-done | bytes 8388624 | tf_op jit(solution)/shard_map/all_gather | solution.py:60
  198.9 17.7 %multiply_convert_fusion.1 = (bf16[290,4096]{1,0:T(8,128)(2,1)}, f32[290,4096]{1,0:T(8,128)}, f32[290,4096]{1,0:T(8,128)}) fusion(f32[4096]{0:T(1024)S(1)} %convert_element_type.150, bf16[1024,4096]{1,0:T(8,128)(2,1)} %all-gather.23.cloned.1.call-done, f32[290,1024]{1,0:T(8,128)S(1)} %get-tuple-element.157, f32[1024]{0:T(1024)S(1)} %bitcast.156, ...), kind=kOutput, calls=%fused_computation.17 | convolution fusion | flops 2512578560 | bytes 21481744 | tf_op jit(solution)/shard_map/dot_general | solution.py:114
  216.6 42.1 %all-gather.25.cloned.1.call-done = bf16[4096,1024]{1,0:T(8,128)(2,1)} async-done(((bf16[1024,1024]{1,0:T(8,128)(2,1)}), bf16[4096,1024]{1,0:T(8,128)(2,1)}) %all-gather.25.cloned.1.call-update) | async-done | bytes 8388624 | tf_op jit(solution)/shard_map/all_gather | solution.py:61
  258.7 10.7 convert_reduce_fusion
  269.3 6.4 multiply_reduce_fusion.1
  288.3 8.7 fusion.13
  297.1 10.0 multiply_reduce_fusion
  307.1 6.5 multiply_convert_fusion
  319.0 125.6 %all-reduce.19 = (bf16[1,580,16,64]{1,3,2,0:T(8,128)(2,1)}, bf16[1,580,16,64]{1,3,2,0:T(8,128)(2,1)}) all-reduce(f32[1,580,16,64]{1,3,2,0:T(8,128)} %fusion.13, f32[1,580,16,64]{1,3,2,0:T(8,128)} %multiply_bitcast_fusion), channel_id=5, replica_groups=mesh['seq'=2,'shard'=4,'rep'=4] {'seq'}, use_global_device_ids=true, to_apply=%region_10.11.clone | all-reduce | flops 1187840 | bytes 7127040
  454.2 9.4 fusion.36
  463.7 13.5 %fusion.59 = f32[1024,4096]{1,0:T(8,128)} fusion(bf16[290,4096]{1,0:T(8,128)(2,1)} %copy-done.18, f32[290,1024]{1,0:T(8,128)S(1)} %get-tuple-element.157, f32[1024]{0:T(1024)S(1)} %bitcast.157, f32[1024]{0:T(1024)S(1)} %bitcast.155, f32[290]{0:T(512)S(1)} %fusion.48, f32[290]{0:T(512)S(1)} %broadcast_multiply_fusion), kind=kOutput, calls=%fused_computation.105 | convolution fusion | flops 2434181120 | bytes 20351248 | tf_op jit(solution)/shard_map/dot_general | solution.py:131
  478.4 10.4 fusion.41
  488.9 73.8 %reduce-scatter.7.cloned.1.call-done = f32[256,3072]{1,0:T(8,128)} async-done(((f32[1024,3072]{1,0:T(8,128)}), f32[256,3072]{1,0:T(8,128)}) %reduce-scatter.7.cloned.1.call-update) | async-done | bytes 3145744 | tf_op jit(solution)/shard_map/reduce_scatter | solution.py:194
  562.7 127.7 %reduce-scatter.11.cloned.1.call-done = f32[256,4096]{1,0:T(8,128)} async-done(((f32[1024,4096]{1,0:T(8,128)}), f32[256,4096]{1,0:T(8,128)}) %reduce-scatter.11.cloned.1.call-update) | async-done | bytes 4194320 | tf_op jit(solution)/shard_map/reduce_scatter | solution.py:203
  690.4 127.5 %reduce-scatter.13.cloned.1.call-done = f32[1024,1024]{1,0:T(8,128)} async-done(((f32[4096,1024]{1,0:T(8,128)}), f32[1024,1024]{1,0:T(8,128)}) %reduce-scatter.13.cloned.1.call-update) | async-done | bytes 4194320 | tf_op jit(solution)/shard_map/reduce_scatter | solution.py:205
  825.8 7.2 fusion.60
  835.4 11.6 all-reduce.13
  851.2 39.8 %all-reduce.11 = (f32[256]{0:T(256)}, f32[256]{0:T(256)}, f32[256]{0:T(256)}, f32[256]{0:T(256)}, f32[256]{0:T(256)}, /*index=5*/f32[256]{0:T(256)}, f32[256]{0:T(256)}, f32[1024]{0:T(1024)}, f32[256]{0:T(256)}) all-reduce(f32[256]{0:T(256)S(1)} %dynamic-slice.7, ...), channel_id=1, replica_groups=mesh['seq'=2,'shard'=4,'rep'=4] {'seq','rep'}, use_global_device_ids=true, to_apply=%region_17.18 | all-reduce | flops 3072 | bytes 24576 | tf_op jit(solution)/shard_map/psum | solution.py:208
  890.9 7.6 fusion.28
  898.6 319.8 %all-reduce.18.cloned.1.call-done = (f32[256,3072]{1,0:T(8,128)}, f32[256,1024]{1,0:T(8,128)}, f32[256,4096]{1,0:T(8,128)}, f32[1024,1024]{1,0:T(8,128)}) async-done(((f32[256,3072]{1,0:T(8,128)}, f32[256,1024]{1,0:T(8,128)}, f32[256,4096]{1,0:T(8,128)}, f32[1024,1024]{1,0:T(8,128)}), (f32[256,3072]{1,0:T(8,128)}, f32[256,1024]{1,0:T(8,128)}, f32[256,4096]{1,0:T(8,128)}, ...) | async-done | bytes 12582928 | tf_op jit(solution)/shard_map/psum | solution.py:208
  (176 shorter events, 133.7 us)
Async XLA Ops:
  7.2 51.5 %all-gather.19.cloned.1.call-start = ((), (), s32[]{:S(2)}) async-start(), calls=%async_computation.4 | async-start | bytes 7864320 | tf_op jit(solution)/shard_map/all_gather | solution.py:58
  7.9 95.6 %all-gather.29.cloned.1.call-start = ((), (), s32[]{:S(2)}) async-start(), calls=%async_computation.13 | async-start | bytes 1818624 | tf_op jit(solution)/shard_map/all_gather | solution.py:84
  23.4 40.5 %copy-start.22 = (f32[290]{0:T(512)}, f32[290]{0:T(512)S(1)}, u32[]{:S(2)}) copy-start(f32[290]{0:T(512)S(1)} %fusion.32) | copy-start | bytes 3484
  58.7 8.1 copy-start.25
  58.7 8.1 copy-start.26
  66.7 48.6 %all-gather.27.cloned.1.call-start = ((), (), s32[]{:S(2)}) async-start(), calls=%async_computation.12 | async-start | bytes 1818624 | tf_op jit(solution)/shard_map/all_gather | solution.py:87
  76.9 20.5 %copy-start.24 = (bf16[1024]{0:T(1024)(128)(2,1)S(1)}, bf16[1024]{0:T(1024)(128)(2,1)}, u32[]{:S(2)}) copy-start(bf16[1024]{0:T(1024)(128)(2,1)} %param.28) | copy-start | bytes 6148
  79.8 59.5 %all-gather.21.cloned.1.call-start = ((), (), s32[]{:S(2)}) async-start(), calls=%async_computation.5 | async-start | bytes 2621440 | tf_op jit(solution)/shard_map/all_gather | solution.py:59
  80.3 118.6 %all-gather.23.cloned.1.call-start = ((), (), s32[]{:S(2)}) async-start(), calls=%async_computation.6 | async-start | bytes 10485760 | tf_op jit(solution)/shard_map/all_gather | solution.py:60
  80.9 177.7 %all-gather.25.cloned.1.call-start = ((), (), s32[]{:S(2)}) async-start(), calls=%async_computation.7 | async-start | bytes 10485760 | tf_op jit(solution)/shard_map/all_gather | solution.py:61
  81.5 407.4 %reduce-scatter.9.cloned.1.call-start = ((), (), s32[]{:S(2)}) async-start(), calls=%async_computation.9 | async-start | bytes 5242880 | tf_op jit(solution)/shard_map/reduce_scatter | solution.py:197
  112.0 14.9 %copy-start.3 = (bf16[580,16,64]{0,2,1:T(8,128)(2,1)}, bf16[580,16,64]{0,2,1:T(8,128)(2,1)S(1)}, u32[]{:S(2)}) copy-start(bf16[580,16,64]{0,2,1:T(8,128)(2,1)S(1)} %reshape.246) | copy-start | bytes 3563524
  269.3 7.9 copy-start.7
  281.7 281.0 %reduce-scatter.7.cloned.1.call-start = ((), (), s32[]{:S(2)}) async-start(), calls=%async_computation.8 | async-start | bytes 15728640 | tf_op jit(solution)/shard_map/reduce_scatter | solution.py:194
  288.3 8.7 copy-start.10
  288.3 18.7 %slice-start = ((s8[12124160]{0:T(1024)(128)(4,1)}), s8[4194304]{0:T(1024)(128)(4,1)S(1)}, s32[]{:S(2)}) async-start(s8[12124160]{0:T(1024)(128)(4,1)} %bitcast.131), calls=%async_computation.15 | async-start | bytes 8388608
  288.3 18.7 %slice-start.1 = ((s8[12124160]{0:T(1024)(128)(4,1)}), s8[4194304]{0:T(1024)(128)(4,1)S(1)}, s32[]{:S(2)}) async-start(s8[12124160]{0:T(1024)(128)(4,1)} %bitcast.131), calls=%async_computation.16 | async-start | bytes 8388608
  297.1 10.0 slice-start.2
  319.0 129.3 %copy-start.4 = (bf16[580,16,64]{0,2,1:T(8,128)(2,1)S(1)}, bf16[580,16,64]{0,2,1:T(8,128)(2,1)}, u32[]{:S(2)}) copy-start(bf16[580,16,64]{0,2,1:T(8,128)(2,1)} %copy-done.3) | copy-start | bytes 3563524
  463.7 226.7 %reduce-scatter.11.cloned.1.call-start = ((), (), s32[]{:S(2)}) async-start(), calls=%async_computation.10 | async-start | bytes 20971520 | tf_op jit(solution)/shard_map/reduce_scatter | solution.py:203
  477.2 340.6 %reduce-scatter.13.cloned.1.call-start = ((), (), s32[]{:S(2)}) async-start(), calls=%async_computation.11 | async-start | bytes 20971520 | tf_op jit(solution)/shard_map/reduce_scatter | solution.py:205
  488.8 729.6 %all-reduce.18.cloned.1.call-start = ((), (), s32[]{:S(2)}) async-start(), calls=%async_computation.14 | async-start | bytes 25165824 | tf_op jit(solution)/shard_map/psum | solution.py:208
  817.9 7.9 copy-start.14
  825.8 7.9 copy-start.6
  (23 other events, 85.3 us)
Sparse Core Ops, SparseCore 0:
  9.5 49.0 all-gather.18
  66.8 23.1 all-gather.28
  92.1 23.1 all-gather.26
  116.6 22.5 all-gather.20
  140.6 58.2 all-gather.22
  200.4 58.2 all-gather.24
  281.8 44.5 reduce-scatter.8
  463.8 98.8 reduce-scatter.6
  565.3 125.0 reduce-scatter.10
  692.8 125.0 reduce-scatter.12
  822.6 395.7 all-reduce.17
where the time goes:
time: 1240 us
  waiting for transfers between devices  792 us (64%)
  blocking collectives  225 us (18%)
  matrix products  130 us (10%)
  local copies, waits for them, and re-layouts  50.5 us (4%)
  other arithmetic  20.7 us (2%)
  between operations  17.2 us (1%)
    psum x1, waiting for transfers between devices, shards(): lax.psum((owned_grads[0], owned_grads[1], owned_grads[2], owned_grads[3],...  320 us
    unnamed x2, blocking collectives  137 us
    reduce_scatter x1, waiting for transfers between devices, shards(): lax.psum_scatter(grad_up, 'shard', scatter_dimension=0, tiled=True)  128 us
    reduce_scatter x1, waiting for transfers between devices, shards(): lax.psum_scatter(grad_down, 'shard', scatter_dimension=0, tiled=True)  128 us
    reduce_scatter x1, waiting for transfers between devices, shards(): lax.psum_scatter(grad_qkv, 'shard', scatter_dimension=0, tiled=True)  73.8 us
    all_gather x1, waiting for transfers between devices, shards(): lax.all_gather(up_weight, 'shard', axis=0, tiled=True)  56.9 us
    all_gather x1, waiting for transfers between devices, shards(): lax.all_gather(down_weight, 'shard', axis=0, tiled=True)  42.1 us
    psum x1, blocking collectives, shards(): lax.psum((owned_grads[0], owned_grads[1], owned_grads[2], owned_grads[3],...  39.8 us
  transfers between devices with their start and end apart: 11, of which 9 were waited for; matrix products, arithmetic and copies ran while one was open for 12% of the time, Pallas kernels for 0%

commit v1 on v0

--- a/solution.py
+++ b/solution.py
@@ -5,6 +5,35 @@
 
 H = 16
 HD = 64
+
+
+def unit_search(axis_id, mine_x):
+    carry, z_new, base_arr = (lax.axis_size(axis_id), lax.axis_index(axis_id), mine_x.shape[0])
+    carry_in = lax.dynamic_update_slice_in_dim(
+        jnp.zeros(
+            tuple((pp * carry if k0 == 0 else pp for k0, pp in enumerate(mine_x.shape))),
+            mine_x.dtype,
+        ),
+        mine_x,
+        z_new * base_arr,
+        axis=0,
+    )
+    odd = local_out = mine_x
+    for m in range(1, carry // 2 + 1):
+        odd = lax.ppermute(odd, axis_id, tuple(((k0, (k0 + 1) % carry) for k0 in range(carry))))
+        carry_in = lax.dynamic_update_slice_in_dim(
+            carry_in, odd, (z_new - m) % carry * base_arr, axis=0
+        )
+        if 2 * m < carry:
+            local_out = lax.ppermute(
+                local_out,
+                axis_name=axis_id,
+                perm=tuple(((k0, (k0 - 1) % carry) for k0 in range(carry))),
+            )
+            carry_in = lax.dynamic_update_slice_in_dim(
+                carry_in, local_out, (z_new + m) % carry * base_arr, axis=0
+            )
+    return carry_in
 
 
 def layer_norm(values, gain_vec, shift_vec):
@@ -55,7 +84,7 @@
     full_len = rows_local * lax.axis_size("seq")
     score_scale = HD ** (-0.5)
     gathered = (
-        lax.all_gather(qkv_weight, "shard", axis=0, tiled=True),
+        unit_search("shard", qkv_weight),
         lax.all_gather(out_weight, "shard", axis=0, tiled=True),
         lax.all_gather(up_weight, "shard", axis=0, tiled=True),
         lax.all_gather(down_weight, "shard", axis=0, tiled=True),

time: 1240 us -> 1310 us (1.056)
  waiting for transfers between devices: 792 us -> 835 us
  blocking collectives: 225 us -> 239 us
    ppermute x0 -> x3, waiting for transfers between devices: none -> 31.4 us  [the longest x2 31.4 us: unit_search(): lax.ppermute(odd, axis_id, tuple(((k0, (k0 + 1) % carry) for k0 in range(...]
    unnamed x97 -> x95, local copies, waits for them, and re-layouts: 28.9 us -> 30.4 us
  transfers between devices with their start and end apart: 11 -> 14, of which waited for: 9 -> 10; matrix products, arithmetic and copies ran while one was open for 12% -> 12% of each run, Pallas kernels for 0% -> 0%
where the time goes in v1:
time: 1310 us; the launch traced here: 1300 us
  waiting for transfers between devices  835 us (64%)
  blocking collectives  239 us (18%)
  matrix products  126 us (10%)
  local copies, waits for them, and re-layouts  58.7 us (4%)
  other arithmetic  20.6 us (2%)
  between operations  17.2 us (1%)
    psum x1, waiting for transfers between devices, shards(): lax.psum((owned_grads[0], owned_grads[1], owned_grads[2], owned_grads[3],...  329 us
    unnamed x2, blocking collectives  137 us
    reduce_scatter x1, waiting for transfers between devices, shards(): lax.psum_scatter(grad_down, 'shard', scatter_dimension=0, tiled=True)  128 us
    reduce_scatter x1, waiting for transfers between devices, shards(): lax.psum_scatter(grad_up, 'shard', scatter_dimension=0, tiled=True)  128 us
    reduce_scatter x1, waiting for transfers between devices, shards(): lax.psum_scatter(grad_qkv, 'shard', scatter_dimension=0, tiled=True)  73 us
    all_gather x1, waiting for transfers between devices, shards(): lax.all_gather(up_weight, 'shard', axis=0, tiled=True)  56.9 us
    all_gather x1, waiting for transfers between devices, shards(): lax.all_gather(down_weight, 'shard', axis=0, tiled=True)  42 us
    psum x1, blocking collectives, shards(): lax.psum((owned_grads[0], owned_grads[1], owned_grads[2], owned_grads[3],...  39.9 us
  transfers between devices with their start and end apart: 14, of which 10 were waited for; matrix products, arithmetic and copies ran while one was open for 12% of the time, Pallas kernels for 0%

profile of v1, /device:TPU:0, one launch (start us, length us, event | category | flops | bytes accessed | tf_op | source)
XLA Modules:
  0.0 1302.2 jit_solution(14568019921382302746)
XLA Ops:
  11.0 31.4 %collective-permute-done = bf16[256,3072]{1,0:T(8,128)(2,1)} collective-permute-done((bf16[256,3072]{1,0:T(8,128)(2,1)}, bf16[256,3072]{1,0:T(8,128)(2,1)}, u32[]{:S(2)}, u32[]{:S(2)}) %collective-permute-start) | collective-permute-done | bytes 1572896 | tf_op jit(solution)/shard_map/ppermute | solution.py:23
  45.5 17.8 %all-gather.2 = bf16[4,1,256]{2,1,0:T(2,128)(2,1)S(1)} all-gather(bf16[1,1,256]{2,1,0:T(2,128)(2,1)S(1)} %reshape.256), channel_id=1, replica_groups=mesh['seq'=2,'shard'=4,'rep'=4] {'shard'}, dimensions={0}, use_global_device_ids=true | all-gather | bytes 2560 | tf_op jit(solution)/shard_map/all_gather | solution.py:94
  64.0 8.0 all-gather.3
  115.5 5.7 all_gather.59
  160.8 56.9 %all-gather.21.cloned.1.call-done = bf16[1024,4096]{1,0:T(8,128)(2,1)} async-done(((bf16[256,4096]{1,0:T(8,128)(2,1)}), bf16[1024,4096]{1,0:T(8,128)(2,1)}) %all-gather.21.cloned.1.call-update) | async-done | bytes 8388624 | tf_op jit(solution)/shard_map/all_gather | solution.py:89
  217.7 17.7 %multiply_convert_fusion.1 = (bf16[290,4096]{1,0:T(8,128)(2,1)}, f32[290,4096]{1,0:T(8,128)}, f32[290,4096]{1,0:T(8,128)}) fusion(f32[4096]{0:T(1024)S(1)} %convert_element_type.150, bf16[1024,4096]{1,0:T(8,128)(2,1)} %all-gather.21.cloned.1.call-done, f32[290,1024]{1,0:T(8,128)S(1)} %get-tuple-element.157, f32[1024]{0:T(1024)S(1)} %bitcast.156, ...), kind=kOutput, calls=%fused_computation.17 | convolution fusion | flops 2512578560 | bytes 21481744 | tf_op jit(solution)/shard_map/dot_general | solution.py:143
  235.3 42.0 %all-gather.23.cloned.1.call-done = bf16[4096,1024]{1,0:T(8,128)(2,1)} async-done(((bf16[1024,1024]{1,0:T(8,128)(2,1)}), bf16[4096,1024]{1,0:T(8,128)(2,1)}) %all-gather.23.cloned.1.call-update) | async-done | bytes 8388624 | tf_op jit(solution)/shard_map/all_gather | solution.py:90
  277.4 10.7 convert_reduce_fusion
  288.0 6.4 multiply_reduce_fusion.1
  307.1 12.6 multiply_reduce_fusion
  321.1 6.5 multiply_convert_fusion
  337.4 125.4 %all-reduce.19 = (bf16[1,580,16,64]{1,3,2,0:T(8,128)(2,1)}, bf16[1,580,16,64]{1,3,2,0:T(8,128)(2,1)}) all-reduce(f32[1,580,16,64]{1,3,2,0:T(8,128)} %fusion.13, f32[1,580,16,64]{1,3,2,0:T(8,128)} %multiply_bitcast_fusion), channel_id=5, replica_groups=mesh['seq'=2,'shard'=4,'rep'=4] {'seq'}, use_global_device_ids=true, to_apply=%region_10.11.clone | all-reduce | flops 1187840 | bytes 7127040
  472.5 9.4 fusion.36
  482.0 13.8 %fusion.59 = f32[1024,4096]{1,0:T(8,128)} fusion(bf16[290,4096]{1,0:T(8,128)(2,1)} %copy-done.17, f32[290,1024]{1,0:T(8,128)S(1)} %get-tuple-element.157, f32[1024]{0:T(1024)S(1)} %bitcast.157, f32[1024]{0:T(1024)S(1)} %bitcast.155, f32[290]{0:T(512)S(1)} %fusion.48, f32[290]{0:T(512)S(1)} %broadcast_multiply_fusion), kind=kOutput, calls=%fused_computation.109 | convolution fusion | flops 2434181120 | bytes 20351248 | tf_op jit(solution)/shard_map/dot_general | solution.py:160
  496.9 10.4 fusion.41
  508.0 73.0 %reduce-scatter.7.cloned.1.call-done = f32[256,3072]{1,0:T(8,128)} async-done(((f32[1024,3072]{1,0:T(8,128)}), f32[256,3072]{1,0:T(8,128)}) %reduce-scatter.7.cloned.1.call-update) | async-done | bytes 3145744 | tf_op jit(solution)/shard_map/reduce_scatter | solution.py:223
  581.0 127.7 %reduce-scatter.11.cloned.1.call-done = f32[256,4096]{1,0:T(8,128)} async-done(((f32[1024,4096]{1,0:T(8,128)}), f32[256,4096]{1,0:T(8,128)}) %reduce-scatter.11.cloned.1.call-update) | async-done | bytes 4194320 | tf_op jit(solution)/shard_map/reduce_scatter | solution.py:232
  708.7 127.7 %reduce-scatter.13.cloned.1.call-done = f32[1024,1024]{1,0:T(8,128)} async-done(((f32[4096,1024]{1,0:T(8,128)}), f32[1024,1024]{1,0:T(8,128)}) %reduce-scatter.13.cloned.1.call-update) | async-done | bytes 4194320 | tf_op jit(solution)/shard_map/reduce_scatter | solution.py:234
  844.3 39.8 %all-gather.25.cloned.1.call-done = bf16[1024,3072]{1,0:T(8,128)(2,1)} async-done(((bf16[256,3072]{1,0:T(8,128)(2,1)}), bf16[1024,3072]{1,0:T(8,128)(2,1)}) %all-gather.25.cloned.1.call-update) | async-done | bytes 6291472 | tf_op jit(solution)/shard_map/all_gather | solution.py:149
  884.1 6.4 fusion.60
  892.9 11.6 all-reduce.13
  908.6 39.9 %all-reduce.11 = (f32[256]{0:T(256)}, f32[256]{0:T(256)}, f32[256]{0:T(256)}, f32[256]{0:T(256)}, f32[256]{0:T(256)}, /*index=5*/f32[256]{0:T(256)}, f32[256]{0:T(256)}, f32[1024]{0:T(1024)}, f32[256]{0:T(256)}) all-reduce(f32[256]{0:T(256)S(1)} %dynamic-slice.7, ...), channel_id=1, replica_groups=mesh['seq'=2,'shard'=4,'rep'=4] {'seq','rep'}, use_global_device_ids=true, to_apply=%region_17.18 | all-reduce | flops 3072 | bytes 24576 | tf_op jit(solution)/shard_map/psum | solution.py:237
  948.5 7.7 fusion.28
  956.2 328.6 %all-reduce.18.cloned.1.call-done = (f32[256,3072]{1,0:T(8,128)}, f32[256,1024]{1,0:T(8,128)}, f32[256,4096]{1,0:T(8,128)}, f32[1024,1024]{1,0:T(8,128)}) async-done(((f32[256,3072]{1,0:T(8,128)}, f32[256,1024]{1,0:T(8,128)}, f32[256,4096]{1,0:T(8,128)}, f32[1024,1024]{1,0:T(8,128)}), (f32[256,3072]{1,0:T(8,128)}, f32[256,1024]{1,0:T(8,128)}, f32[256,4096]{1,0:T(8,128)}, ...) | async-done | bytes 12582928 | tf_op jit(solution)/shard_map/psum | solution.py:237
  (185 shorter events, 148.2 us)
Async XLA Ops:
  7.2 67.0 %copy-start.6 = (bf16[256,3072]{1,0:T(8,128)(2,1)S(1)}, bf16[256,3072]{1,0:T(8,128)(2,1)}, u32[]{:S(2)}) copy-start(bf16[256,3072]{1,0:T(8,128)(2,1)} %param.18) | copy-start | bytes 4718596
  7.2 114.4 %all-gather.29.cloned.1.call-start = ((), (), s32[]{:S(2)}) async-start(), calls=%async_computation.13 | async-start | bytes 1818624 | tf_op jit(solution)/shard_map/all_gather | solution.py:113
  7.2 35.1 %collective-permute-start = (bf16[256,3072]{1,0:T(8,128)(2,1)}, bf16[256,3072]{1,0:T(8,128)(2,1)}, u32[]{:S(2)}, u32[]{:S(2)}) collective-permute-start(bf16[256,3072]{1,0:T(8,128)(2,1)} %param.18), channel_id=1, source_target_pairs={{0,4},{4,8},{8,12},{12,0},{1,5},{5,9},{9,13},{13,1},{2,6},{6,10},{... | collective-permute-start | bytes 4718600 | tf_op jit(solution)/shard_map/ppermute | solution.py:23
  7.8 68.3 %collective-permute-start.1 = (bf16[256,3072]{1,0:T(8,128)(2,1)}, bf16[256,3072]{1,0:T(8,128)(2,1)}, u32[]{:S(2)}, u32[]{:S(2)}) collective-permute-start(bf16[256,3072]{1,0:T(8,128)(2,1)} %param.18), channel_id=1, source_target_pairs={{0,12},{4,0},{8,4},{12,8},{1,13},{5,1},{9,5},{13,9},{2,14},{6,2},{... | collective-permute-start | bytes 4718600 | tf_op jit(solution)/shard_map/ppermute | solution.py:28
  42.4 35.3 %collective-permute-start.2 = (bf16[256,3072]{1,0:T(8,128)(2,1)}, bf16[256,3072]{1,0:T(8,128)(2,1)}, u32[]{:S(2)}, u32[]{:S(2)}) collective-permute-start(bf16[256,3072]{1,0:T(8,128)(2,1)} %collective-permute-done), channel_id=1, source_target_pairs={{0,4},{4,8},{8,12},{12,0},{1,5},{5,9},{9,13},{13,1},{2,6},{6,10},{... | collective-permute-start | bytes 4718600 | tf_op jit(solution)/shard_map/ppermute | solution.py:23
  84.4 49.4 %all-gather.27.cloned.1.call-start = ((), (), s32[]{:S(2)}) async-start(), calls=%async_computation.12 | async-start | bytes 1818624 | tf_op jit(solution)/shard_map/all_gather | solution.py:116
  94.8 10.6 copy-start.27
  94.8 15.6 %copy-start.28 = (bf16[256]{0:T(256)(128)(2,1)S(1)}, bf16[256]{0:T(256)(128)(2,1)}, u32[]{:S(2)}) copy-start(bf16[256]{0:T(256)(128)(2,1)} %param.26) | copy-start | bytes 1540
  94.8 20.7 %copy-start.23 = (bf16[1024]{0:T(1024)(128)(2,1)S(1)}, bf16[1024]{0:T(1024)(128)(2,1)}, u32[]{:S(2)}) copy-start(bf16[1024]{0:T(1024)(128)(2,1)} %param.28) | copy-start | bytes 6148
  97.6 60.3 %all-gather.19.cloned.1.call-start = ((), (), s32[]{:S(2)}) async-start(), calls=%async_computation.4 | async-start | bytes 2621440 | tf_op jit(solution)/shard_map/all_gather | solution.py:88
  98.4 119.3 %all-gather.21.cloned.1.call-start = ((), (), s32[]{:S(2)}) async-start(), calls=%async_computation.5 | async-start | bytes 10485760 | tf_op jit(solution)/shard_map/all_gather | solution.py:89
  98.9 178.4 %all-gather.23.cloned.1.call-start = ((), (), s32[]{:S(2)}) async-start(), calls=%async_computation.6 | async-start | bytes 10485760 | tf_op jit(solution)/shard_map/all_gather | solution.py:90
  99.5 408.4 %reduce-scatter.9.cloned.1.call-start = ((), (), s32[]{:S(2)}) async-start(), calls=%async_computation.9 | async-start | bytes 5242880 | tf_op jit(solution)/shard_map/reduce_scatter | solution.py:226
  300.4 280.7 %reduce-scatter.7.cloned.1.call-start = ((), (), s32[]{:S(2)}) async-start(), calls=%async_computation.8 | async-start | bytes 15728640 | tf_op jit(solution)/shard_map/reduce_scatter | solution.py:223
  307.0 12.6 slice-start
  307.0 12.6 slice-start.1
  307.0 14.1 %slice-start.2 = ((s8[12124160]{0:T(1024)(128)(4,1)}), s8[3735552]{0:T(1024)(128)(4,1)S(1)}, s32[]{:S(2)}) async-start(s8[12124160]{0:T(1024)(128)(4,1)} %bitcast.131), calls=%async_computation.17 | async-start | bytes 7471104
  337.4 129.2 %copy-start.3 = (bf16[580,16,64]{0,2,1:T(8,128)(2,1)S(1)}, bf16[580,16,64]{0,2,1:T(8,128)(2,1)}, u32[]{:S(2)}) copy-start(bf16[580,16,64]{0,2,1:T(8,128)(2,1)} %reshape.246) | copy-start | bytes 3563524
  481.9 226.8 %reduce-scatter.11.cloned.1.call-start = ((), (), s32[]{:S(2)}) async-start(), calls=%async_computation.10 | async-start | bytes 20971520 | tf_op jit(solution)/shard_map/reduce_scatter | solution.py:232
  495.7 340.6 %reduce-scatter.13.cloned.1.call-start = ((), (), s32[]{:S(2)}) async-start(), calls=%async_computation.11 | async-start | bytes 20971520 | tf_op jit(solution)/shard_map/reduce_scatter | solution.py:234
  507.3 376.8 %all-gather.25.cloned.1.call-start = ((), (), s32[]{:S(2)}) async-start(), calls=%async_computation.7 | async-start | bytes 7864320 | tf_op jit(solution)/shard_map/all_gather | solution.py:149
  507.9 776.9 %all-reduce.18.cloned.1.call-start = ((), (), s32[]{:S(2)}) async-start(), calls=%async_computation.14 | async-start | bytes 25165824 | tf_op jit(solution)/shard_map/psum | solution.py:237
  844.3 46.3 %copy-start.22 = (f32[290]{0:T(512)S(1)}, f32[290]{0:T(512)}, u32[]{:S(2)}) copy-start(f32[290]{0:T(512)} %copy-done.21) | copy-start | bytes 3484
  844.3 47.0 %copy-start.5 = (f32[290,1024]{1,0:T(8,128)S(1)}, f32[290,1024]{1,0:T(8,128)}, u32[]{:S(2)}) copy-start(f32[290,1024]{1,0:T(8,128)} %copy-done.4) | copy-start | bytes 3563524
  (25 other events, 96.3 us)
Sparse Core Ops, SparseCore 0:
  84.5 23.9 all-gather.28
  110.6 23.1 all-gather.26
  135.4 22.5 all-gather.18
  159.4 58.2 all-gather.20
  219.1 58.2 all-gather.22
  300.5 44.5 reduce-scatter.8
  482.0 98.9 reduce-scatter.6
  583.6 125.0 reduce-scatter.10
  711.3 125.0 reduce-scatter.12
  837.8 46.3 all-gather.24
  888.9 395.8 all-reduce.17
